TPU v7x, 256 devices: a whole 4x4x8 slice. The times are simulated.
256 devices in a mesh: tm: 8 (over y_hi, x), cells: 32 (over z, y_lo, core).
Axes of the slice: x: 4, y: 4 (y_hi: 2, y_lo: 2; y = y_hi * 2 + y_lo), z: 8, core: 2. Of those that a mesh axis runs over, the one named last changes fastest.
Arguments:
- footprint: float32 [8, 4, 768, 8192], P('tm', None, None, 'cells'), may hold values from -0.03125 to 0.03125
- flux: float32 [8, 8192, 2048], P('tm', 'cells'), may hold values from -6 to 6
- obs_weight: float32 [8, 768], P('tm'), may hold values from 0.2 to 5
- obs_count: int32 [8], P('tm'), may hold values from 1 to 768, 4608 in all
Outputs:
- normal_image: float32 [8, 8192, 2048], P('tm', 'cells')
Inputs may be any that keep to these rules, and one draw needn't show every extreme that they name: `obs_count`: each block has at least one valid slot; one block has all 768 slots valid.
All inputs are finite; a program needn't handle non-finite values.
Results may differ from a plain program's by a relative error of at most 0.0001.
Values sent between devices are 32-bit elements; how exact they have to be, the bound alone decides.
A program may use at most 128 MiB of HBM per device.

v0:
```python
import jax
import jax.numpy as jnp
from jax import lax
from jax.sharding import Mesh
from jax.sharding import PartitionSpec as P

CELLS = ("cells_0", "cells_1", "cells_2")


def from_behind(value, axis, by):
    devices = lax.axis_size(axis)
    pairs = [(i, i + by) for i in range(devices) if 0 <= i + by < devices]
    return lax.ppermute(value, axis, pairs)


def padded_to(lines, devices):
    spare = -lines.shape[0] % devices
    if not spare:
        return lines
    return jnp.concatenate([lines, jnp.zeros((spare, *lines.shape[1:]), lines.dtype)])


def nested_sum(value, near, far):
    lines = value.reshape(-1, *value.shape[1:][-1:])
    padded = padded_to(lines, lax.axis_size(near))
    own = lax.psum_scatter(padded, near, scatter_dimension=0, tiled=True)
    own = lax.psum(own, far)
    whole = lax.all_gather(own, near, axis=0, tiled=True)
    return whole[: len(lines)].reshape(value.shape)


def on_device(footprint, flux, obs_weight, obs_count):
    highest = lax.Precision.HIGHEST
    foot_slab = footprint[0]
    own_flux = flux[0]
    lag_count = foot_slab.shape[0]
    slot_count = foot_slab.shape[1]
    earlier = [own_flux]
    for lag_step in range(1, lag_count):
        earlier.append(from_behind(own_flux, "tm", lag_step))
    valid_rows = (jnp.arange(slot_count, dtype=jnp.int32) < obs_count[0]).astype(jnp.float32)
    row_scale = valid_rows * obs_weight[0]
    partial_value = jnp.dot(
        foot_slab[0], earlier[0], precision=highest, preferred_element_type=jnp.float32
    )
    for lag_step in range(1, lag_count):
        partial_value = partial_value + jnp.dot(
            foot_slab[lag_step],
            earlier[lag_step],
            precision=highest,
            preferred_element_type=jnp.float32,
        )
    modelled = nested_sum(partial_value, "cells_2", ("cells_0", "cells_1"))
    weighted = row_scale[:, None] * modelled
    adjoint_terms = []
    for lag_step in range(lag_count):
        adjoint_terms.append(
            lax.dot_general(
                foot_slab[lag_step],
                weighted,
                (((0,), (0,)), ((), ())),
                precision=highest,
                preferred_element_type=jnp.float32,
            )
        )
    accumulator = adjoint_terms[0]
    for lag_step in range(1, lag_count):
        accumulator = accumulator + from_behind(adjoint_terms[lag_step], "tm", -lag_step)
    return accumulator[None]


def solution(mesh):
    torus = Mesh(
        mesh.devices.reshape(mesh.shape["tm"], 8, 2, 2), ("tm", "cells_0", "cells_1", "cells_2")
    )
    placed = (P("tm", None, None, CELLS), P("tm", CELLS, None), P("tm", None), P("tm"))
    return jax.shard_map(
        on_device, mesh=torus, in_specs=placed, out_specs=P("tm", CELLS, None), check_vma=False
    )
```

profile of v0, /device:TPU:6, one launch (start us, length us, event | category | flops | bytes accessed | tf_op | source)
XLA Modules:
  0.0 543.6 jit_solution(7691611369154677838)
XLA Ops:
  6.5 0.0 reduce-scatter.2.cloned.1.call-start
  6.5 0.0 copy-start.1
  6.5 6.2 %collective-permute-start.1 = (f32[256,2048]{1,0:T(8,128)}, f32[256,2048]{1,0:T(8,128)S(1)}, u32[]{:S(2)}, u32[]{:S(2)}) collective-permute-start(f32[256,2048]{1,0:T(8,128)} %bitcast.48), channel_id=1, source_target_pairs={{0,64},{32,96},{64,128},{96,160},{128,192},{160,224},{1,65},{33,97... | collective-permute-start | bytes 6291464 | tf_op jit(solution)/shard_map/ppermute | solution.py:13
  12.7 4.0 collective-permute-start
  16.8 1.9 collective-permute-start.2
  18.7 7.0 %fusion.48 = f32[768,2048]{1,0:T(8,128)S(1)} fusion(f32[1,4,768,256]{3,2,1,0:T(8,128)} %param.4, f32[1,256,2048]{2,1,0:T(8,128)} %param.5), kind=kOutput, calls=%fused_computation.31 | convolution fusion | flops 4831838208 | bytes 9175040 | tf_op jit(solution)/shard_map/dot_general | solution.py:43
  25.7 33.4 %collective-permute-done.1 = f32[256,2048]{1,0:T(8,128)S(1)} collective-permute-done((f32[256,2048]{1,0:T(8,128)}, f32[256,2048]{1,0:T(8,128)S(1)}, u32[]{:S(2)}, u32[]{:S(2)}) %collective-permute-start.1) | collective-permute-done | bytes 2097184 | tf_op jit(solution)/shard_map/ppermute | solution.py:13
  59.1 0.0 copy-done.1
  59.1 5.1 fusion.42
  64.3 68.4 %collective-permute-done = f32[256,2048]{1,0:T(8,128)S(1)} collective-permute-done((f32[256,2048]{1,0:T(8,128)}, f32[256,2048]{1,0:T(8,128)S(1)}, u32[]{:S(2)}, u32[]{:S(2)}) %collective-permute-start) | collective-permute-done | bytes 2097184 | tf_op jit(solution)/shard_map/ppermute | solution.py:13
  132.7 5.3 fusion.45
  138.0 0.0 collective-permute-done.2
  138.0 7.8 %add_add_fusion = f32[768,2048]{1,0:T(8,128)} fusion(f32[768,2048]{1,0:T(8,128)S(1)} %fusion.42, f32[768,2048]{1,0:T(8,128)S(1)} %fusion.48, f32[768,2048]{1,0:T(8,128)S(1)} %fusion.45, f32[256,2048]{1,0:T(8,128)S(1)} %collective-permute-done.2, f32[1,4,768,256]{3,2,1,0:T(8,128)S(1)} %copy-done.1), kind=kOutput, calls=%fused_computation | convolution fusion | flops 4836556800 | bytes 28049408 | tf_op jit(solution)/shard_map/dot_general | solution.py:47
  145.8 0.0 reduce-scatter.2.cloned.1.call-update
  145.9 0.0 all-reduce.2.cloned.1.call-start
  145.9 32.8 %reduce-scatter.2.cloned.1.call-done = f32[384,2048]{1,0:T(8,128)} async-done(((f32[768,2048]{1,0:T(8,128)}), f32[384,2048]{1,0:T(8,128)}) %reduce-scatter.2.cloned.1.call-update) | async-done | bytes 3145744 | tf_op jit(solution)/shard_map/reduce_scatter | solution.py:26
  178.7 0.0 copy-start.2
  178.7 0.0 all-reduce.2.cloned.1.call-update
  178.7 0.0 all-gather.2.cloned.1.call-start
  178.8 166.7 %all-reduce.2.cloned.1.call-done = f32[384,2048]{1,0:T(8,128)} async-done(((f32[384,2048]{1,0:T(8,128)}), f32[384,2048]{1,0:T(8,128)}) %all-reduce.2.cloned.1.call-update) | async-done | bytes 3145744 | tf_op jit(solution)/shard_map/psum | solution.py:27
  345.4 0.0 all-gather.2.cloned.1.call-update
  346.1 0.0 copy-done.2
  346.2 20.5 %all-gather.2.cloned.1.call-done = f32[768,2048]{1,0:T(8,128)} async-done(((f32[384,2048]{1,0:T(8,128)}), f32[768,2048]{1,0:T(8,128)}) %all-gather.2.cloned.1.call-update) | async-done | bytes 6291472 | tf_op jit(solution)/shard_map/all_gather | solution.py:28
  366.7 0.0 copy-start
  366.7 12.4 %fusion.15 = f32[256,2048]{0,1:T(8,128)S(1)} fusion(f32[768,2048]{1,0:T(8,128)} %all-gather.2.cloned.1.call-done, f32[768]{0:T(1024)S(1)} %fusion.58, f32[1,4,768,256]{3,2,1,0:T(8,128)S(1)} %copy-done.1), kind=kOutput, calls=%fused_computation.14 | convolution fusion | flops 4833411072 | bytes 9179136 | tf_op jit(solution)/shard_map/dot_general | solution.py:58
  379.2 3.0 collective-permute-start.3
  382.1 0.0 copy-done
  382.1 10.4 %fusion.18 = f32[256,2048]{0,1:T(8,128)S(1)} fusion(f32[768,2048]{1,0:T(8,128)S(1)} %copy-done, f32[768]{0:T(1024)S(1)} %fusion.58, f32[1,4,768,256]{3,2,1,0:T(8,128)S(1)} %copy-done.1), kind=kOutput, calls=%fused_computation.15 | convolution fusion | flops 4833411072 | bytes 9179136 | tf_op jit(solution)/shard_map/dot_general | solution.py:58
  392.6 3.7 collective-permute-start.4
  396.3 10.4 %fusion.21 = f32[256,2048]{0,1:T(8,128)S(1)} fusion(f32[768,2048]{1,0:T(8,128)S(1)} %copy-done, f32[768]{0:T(1024)S(1)} %fusion.58, f32[1,4,768,256]{3,2,1,0:T(8,128)S(1)} %copy-done.1), kind=kOutput, calls=%fused_computation.16 | convolution fusion | flops 4833411072 | bytes 9179136 | tf_op jit(solution)/shard_map/dot_general | solution.py:58
  406.8 2.1 collective-permute-start.5
  408.9 88.0 %collective-permute-done.3 = f32[256,2048]{0,1:T(8,128)S(1)} collective-permute-done((f32[256,2048]{0,1:T(8,128)S(1)}, f32[256,2048]{0,1:T(8,128)S(1)}, u32[]{:S(2)}, u32[]{:S(2)}) %collective-permute-start.3) | collective-permute-done | bytes 2097184 | tf_op jit(solution)/shard_map/ppermute | solution.py:13
  496.9 0.0 collective-permute-done.4
  496.9 25.5 %collective-permute-done.5 = f32[256,2048]{0,1:T(8,128)S(1)} collective-permute-done((f32[256,2048]{0,1:T(8,128)S(1)}, f32[256,2048]{0,1:T(8,128)S(1)}, u32[]{:S(2)}, u32[]{:S(2)}) %collective-permute-start.5) | collective-permute-done | bytes 2097184 | tf_op jit(solution)/shard_map/ppermute | solution.py:13
  522.4 11.7 %fusion.33 = f32[1,256,2048]{1,2,0:T(8,128)} fusion(f32[256,2048]{0,1:T(8,128)S(1)} %collective-permute-done.5, f32[256,2048]{0,1:T(8,128)S(1)} %collective-permute-done.4, f32[256,2048]{0,1:T(8,128)S(1)} %collective-permute-done.3, f32[768,2048]{1,0:T(8,128)S(1)} %copy-done, f32[768]{0:T(1024)S(1)} %fusion.58, f32[1,4,768,256]{3,2,1,0:T(8,128)S(1)} %copy-done.1), kind=kOutput, calls=%fused_computation.20 | convolution fusion | flops 4834983936 | bytes 15470592 | tf_op jit(solution)/shard_map/dot_general | solution.py:58
  534.0 2.9 copy.5
  (2 shorter events, 0.0 us)
Async XLA Ops:
  6.5 172.2 %reduce-scatter.2.cloned.1.call-start = ((), (), s32[]{:S(2)}) async-start(), calls=%async_computation.1 | async-start | bytes 9437184 | tf_op jit(solution)/shard_map/reduce_scatter | solution.py:26
  6.5 52.6 %copy-start.1 = (f32[1,4,768,256]{3,2,1,0:T(8,128)S(1)}, f32[1,4,768,256]{3,2,1,0:T(8,128)}, u32[]{:S(2)}) copy-start(f32[1,4,768,256]{3,2,1,0:T(8,128)} %param.4) | copy-start | bytes 9437188
  6.5 52.6 %collective-permute-start.1 = (f32[256,2048]{1,0:T(8,128)}, f32[256,2048]{1,0:T(8,128)S(1)}, u32[]{:S(2)}, u32[]{:S(2)}) collective-permute-start(f32[256,2048]{1,0:T(8,128)} %bitcast.48), channel_id=1, source_target_pairs={{0,64},{32,96},{64,128},{96,160},{128,192},{160,224},{1,65},{33,97... | collective-permute-start | bytes 6291464 | tf_op jit(solution)/shard_map/ppermute | solution.py:13
  12.7 119.9 %collective-permute-start = (f32[256,2048]{1,0:T(8,128)}, f32[256,2048]{1,0:T(8,128)S(1)}, u32[]{:S(2)}, u32[]{:S(2)}) collective-permute-start(f32[256,2048]{1,0:T(8,128)} %bitcast.49), channel_id=1, source_target_pairs={{0,32},{32,64},{64,96},{96,128},{128,160},{160,192},{192,224},{1,3... | collective-permute-start | bytes 6291464 | tf_op jit(solution)/shard_map/ppermute | solution.py:13
  16.8 121.3 %collective-permute-start.2 = (f32[256,2048]{1,0:T(8,128)}, f32[256,2048]{1,0:T(8,128)S(1)}, u32[]{:S(2)}, u32[]{:S(2)}) collective-permute-start(f32[256,2048]{1,0:T(8,128)} %bitcast.50), channel_id=1, source_target_pairs={{0,96},{32,128},{64,160},{96,192},{128,224},{1,97},{33,129},{65,16... | collective-permute-start | bytes 6291464 | tf_op jit(solution)/shard_map/ppermute | solution.py:13
  145.9 199.6 %all-reduce.2.cloned.1.call-start = ((), (), s32[]{:S(2)}) async-start(), calls=%async_computation.2 | async-start | bytes 6291456 | tf_op jit(solution)/shard_map/psum | solution.py:27
  178.7 167.4 %copy-start.2 = (f32[1,768]{1,0:T(1,128)S(1)}, f32[1,768]{1,0:T(1,128)}, u32[]{:S(2)}) copy-start(f32[1,768]{1,0:T(1,128)} %param.6) | copy-start | bytes 9220
  178.7 188.0 %all-gather.2.cloned.1.call-start = ((), (), s32[]{:S(2)}) async-start(), calls=%async_computation.3 | async-start | bytes 9437184 | tf_op jit(solution)/shard_map/all_gather | solution.py:28
  366.7 15.4 %copy-start = (f32[768,2048]{1,0:T(8,128)S(1)}, f32[768,2048]{1,0:T(8,128)}, u32[]{:S(2)}) copy-start(f32[768,2048]{1,0:T(8,128)} %all-gather.2.cloned.1.call-done) | copy-start | bytes 18874372
  379.2 117.8 %collective-permute-start.3 = (f32[256,2048]{0,1:T(8,128)S(1)}, f32[256,2048]{0,1:T(8,128)S(1)}, u32[]{:S(2)}, u32[]{:S(2)}) collective-permute-start(f32[256,2048]{0,1:T(8,128)S(1)} %fusion.15), channel_id=1, source_target_pairs={{32,0},{64,32},{96,64},{128,96},{160,128},{192,160},{224,192},{33,... | collective-permute-start | bytes 6291464 | tf_op jit(solution)/shard_map/ppermute | solution.py:13
  392.6 104.3 %collective-permute-start.4 = (f32[256,2048]{0,1:T(8,128)S(1)}, f32[256,2048]{0,1:T(8,128)S(1)}, u32[]{:S(2)}, u32[]{:S(2)}) collective-permute-start(f32[256,2048]{0,1:T(8,128)S(1)} %fusion.18), channel_id=1, source_target_pairs={{64,0},{96,32},{128,64},{160,96},{192,128},{224,160},{65,1},{97,33... | collective-permute-start | bytes 6291464 | tf_op jit(solution)/shard_map/ppermute | solution.py:13
  406.8 115.6 %collective-permute-start.5 = (f32[256,2048]{0,1:T(8,128)S(1)}, f32[256,2048]{0,1:T(8,128)S(1)}, u32[]{:S(2)}, u32[]{:S(2)}) collective-permute-start(f32[256,2048]{0,1:T(8,128)S(1)} %fusion.21), channel_id=1, source_target_pairs={{96,0},{128,32},{160,64},{192,96},{224,128},{97,1},{129,33},{161,6... | collective-permute-start | bytes 6291464 | tf_op jit(solution)/shard_map/ppermute | solution.py:13
Sparse Core Ops, SparseCore 0:
  146.0 32.6 reduce-scatter.1
  181.4 164.0 all-reduce.1
  347.2 19.4 all-gather.1
where the time goes:
time: 553 us; the launch traced here: 544 us
  waiting for transfers between devices  435 us (79%)
  matrix products  70.3 us (13%)
  starting transfers between devices  21 us (4%)
  between operations  14.1 us (3%)
    ppermute x6, waiting for transfers between devices, from_behind(): return lax.ppermute(value, axis, pairs)  215 us
    psum x1, waiting for transfers between devices, nested_sum(): own = lax.psum(own, far)  167 us
    dot_general x4, matrix products, on_device(): lax.dot_general(foot_slab[lag_step], weighted, (((0,), (0,)), ((), ())),...  45 us
    reduce_scatter x1, waiting for transfers between devices, nested_sum(): own = lax.psum_scatter(padded, near, scatter_dimension=0, tiled=True)  32.8 us
    ppermute x6, starting transfers between devices, from_behind(): return lax.ppermute(value, axis, pairs)  20.9 us
    all_gather x1, waiting for transfers between devices, nested_sum(): whole = lax.all_gather(own, near, axis=0, tiled=True)  20.5 us
    dot_general x3, matrix products, on_device(): jnp.dot(foot_slab[lag_step], earlier[lag_step], precision=highest, prefer...  18.3 us
  transfers between devices with their start and end apart: 9, of which 7 were waited for; matrix products, arithmetic and copies ran while one was open for 7% of the time, Pallas kernels for 0%

commit v1 on v0

--- a/solution.py
+++ b/solution.py
@@ -24,7 +24,8 @@
     lines = value.reshape(-1, *value.shape[1:][-1:])
     padded = padded_to(lines, lax.axis_size(near))
     own = lax.psum_scatter(padded, near, scatter_dimension=0, tiled=True)
-    own = lax.psum(own, far)
+    blocks = lax.all_gather(own, far, axis=0, tiled=False)
+    own = blocks.sum(axis=0)
     whole = lax.all_gather(own, near, axis=0, tiled=True)
     return whole[: len(lines)].reshape(value.shape)
 

time: 553 us -> 1440 us (2.60)
  waiting for transfers between devices: 435 us -> 1300 us
  other arithmetic: 0.02 us -> 18.8 us
    all_gather x0 -> x1, waiting for transfers between devices: none -> 1030 us  [nested_sum(): blocks = lax.all_gather(own, far, axis=0, tiled=False)]
    psum x1 -> x0, waiting for transfers between devices: 167 us -> none  [nested_sum(): own = lax.psum(own, far)]
    reduce_sum x0 -> x1, other arithmetic: none -> 18.8 us  [nested_sum(): own = blocks.sum(axis=0)]
  transfers between devices with their start and end apart: 9 -> 9, of which waited for: 7 -> 7; matrix products, arithmetic and copies ran while one was open for 7% -> 3% of each run, Pallas kernels for 0% -> 0%
where the time goes in v1:
time: 1440 us; the launch traced here: 1430 us
  waiting for transfers between devices  1300 us (90%)
  matrix products  70.3 us (5%)
  starting transfers between devices  21 us (1%)
  other arithmetic  18.8 us (1%)
    all_gather x1, waiting for transfers between devices, nested_sum(): blocks = lax.all_gather(own, far, axis=0, tiled=False)  1030 us
    ppermute x6, waiting for transfers between devices, from_behind(): return lax.ppermute(value, axis, pairs)  215 us
    dot_general x4, matrix products, on_device(): lax.dot_general(foot_slab[lag_step], weighted, (((0,), (0,)), ((), ())),...  45 us
    reduce_scatter x1, waiting for transfers between devices, nested_sum(): own = lax.psum_scatter(padded, near, scatter_dimension=0, tiled=True)  32.8 us
  transfers between devices with their start and end apart: 9, of which 7 were waited for; matrix products, arithmetic and copies ran while one was open for 3% of the time, Pallas kernels for 0%

profile of v1, /device:TPU:6, one launch (start us, length us, event | category | flops | bytes accessed | tf_op | source)
XLA Modules:
  0.0 1425.8 jit_solution(5210181963360276627)
XLA Ops:
  6.5 0.0 reduce-scatter.2.cloned.1.call-start
  6.5 0.0 copy-start.1
  6.5 6.2 collective-permute-start.1
  12.7 4.0 collective-permute-start
  16.8 1.9 collective-permute-start.2
  18.7 7.0 fusion.48
  25.7 33.4 %collective-permute-done.1 = f32[256,2048]{1,0:T(8,128)S(1)} collective-permute-done((f32[256,2048]{1,0:T(8,128)}, f32[256,2048]{1,0:T(8,128)S(1)}, u32[]{:S(2)}, u32[]{:S(2)}) %collective-permute-start.1) | collective-permute-done | bytes 2097184 | tf_op jit(solution)/shard_map/ppermute | solution.py:13
  59.1 0.0 copy-done.1
  59.1 5.1 fusion.42
  64.3 68.4 %collective-permute-done = f32[256,2048]{1,0:T(8,128)S(1)} collective-permute-done((f32[256,2048]{1,0:T(8,128)}, f32[256,2048]{1,0:T(8,128)S(1)}, u32[]{:S(2)}, u32[]{:S(2)}) %collective-permute-start) | collective-permute-done | bytes 2097184 | tf_op jit(solution)/shard_map/ppermute | solution.py:13
  132.7 5.3 fusion.45
  138.0 0.0 collective-permute-done.2
  138.0 7.8 add_add_fusion
  145.8 0.0 reduce-scatter.2.cloned.1.call-update
  145.9 0.0 all-gather.6.cloned.1.call-start
  145.9 32.8 %reduce-scatter.2.cloned.1.call-done = f32[384,2048]{1,0:T(8,128)} async-done(((f32[768,2048]{1,0:T(8,128)}), f32[384,2048]{1,0:T(8,128)}) %reduce-scatter.2.cloned.1.call-update) | async-done | bytes 3145744 | tf_op jit(solution)/shard_map/reduce_scatter | solution.py:26
  178.7 0.0 all-gather.6.cloned.1.call-update
  178.7 0.0 all-gather.4.cloned.1.call-start
  178.8 1028.1 %all-gather.6.cloned.1.call-done = f32[6144,2048]{1,0:T(8,128)} async-done(((f32[384,2048]{1,0:T(8,128)}), f32[6144,2048]{1,0:T(8,128)}) %all-gather.6.cloned.1.call-update) | async-done | bytes 50331664 | tf_op jit(solution)/shard_map/all_gather | solution.py:27
  1206.9 18.8 %reduce_sum.9 = f32[384,2048]{1,0:T(8,128)} reduce(f32[16,384,2048]{2,1,0:T(8,128)} %bitcast.49, f32[]{:T(128)} %constant.2.clone.1), dimensions={0}, to_apply=%region_1.0 | reduce | flops 11796480 | bytes 53477380 | tf_op jit(solution)/shard_map/reduce_sum | solution.py:28
  1225.7 0.0 copy-start.2
  1225.7 0.0 all-gather.4.cloned.1.call-update
  1226.4 0.0 copy-done.2
  1226.4 22.5 %all-gather.4.cloned.1.call-done = f32[768,2048]{1,0:T(8,128)} async-done(((f32[384,2048]{1,0:T(8,128)}), f32[768,2048]{1,0:T(8,128)}) %all-gather.4.cloned.1.call-update) | async-done | bytes 6291472 | tf_op jit(solution)/shard_map/all_gather | solution.py:29
  1248.9 0.0 copy-start
  1248.9 12.4 fusion.15
  1261.3 3.0 collective-permute-start.3
  1264.3 0.0 copy-done
  1264.3 10.4 fusion.18
  1274.8 3.7 collective-permute-start.4
  1278.5 10.4 fusion.21
  1289.0 2.1 collective-permute-start.5
  1291.1 88.0 %collective-permute-done.3 = f32[256,2048]{0,1:T(8,128)S(1)} collective-permute-done((f32[256,2048]{0,1:T(8,128)S(1)}, f32[256,2048]{0,1:T(8,128)S(1)}, u32[]{:S(2)}, u32[]{:S(2)}) %collective-permute-start.3) | collective-permute-done | bytes 2097184 | tf_op jit(solution)/shard_map/ppermute | solution.py:13
  1379.1 0.0 collective-permute-done.4
  1379.1 25.5 %collective-permute-done.5 = f32[256,2048]{0,1:T(8,128)S(1)} collective-permute-done((f32[256,2048]{0,1:T(8,128)S(1)}, f32[256,2048]{0,1:T(8,128)S(1)}, u32[]{:S(2)}, u32[]{:S(2)}) %collective-permute-start.5) | collective-permute-done | bytes 2097184 | tf_op jit(solution)/shard_map/ppermute | solution.py:13
  1404.6 11.7 fusion.33
  1416.2 2.9 copy.5
  (2 shorter events, 0.0 us)
Async XLA Ops:
  6.5 172.2 %reduce-scatter.2.cloned.1.call-start = ((), (), s32[]{:S(2)}) async-start(), calls=%async_computation.1 | async-start | bytes 9437184 | tf_op jit(solution)/shard_map/reduce_scatter | solution.py:26
  6.5 52.6 %copy-start.1 = (f32[1,4,768,256]{3,2,1,0:T(8,128)S(1)}, f32[1,4,768,256]{3,2,1,0:T(8,128)}, u32[]{:S(2)}) copy-start(f32[1,4,768,256]{3,2,1,0:T(8,128)} %param.4) | copy-start | bytes 9437188
  6.5 52.6 %collective-permute-start.1 = (f32[256,2048]{1,0:T(8,128)}, f32[256,2048]{1,0:T(8,128)S(1)}, u32[]{:S(2)}, u32[]{:S(2)}) collective-permute-start(f32[256,2048]{1,0:T(8,128)} %bitcast.50), channel_id=1, source_target_pairs={{0,64},{32,96},{64,128},{96,160},{128,192},{160,224},{1,65},{33,97... | collective-permute-start | bytes 6291464 | tf_op jit(solution)/shard_map/ppermute | solution.py:13
  12.7 119.9 %collective-permute-start = (f32[256,2048]{1,0:T(8,128)}, f32[256,2048]{1,0:T(8,128)S(1)}, u32[]{:S(2)}, u32[]{:S(2)}) collective-permute-start(f32[256,2048]{1,0:T(8,128)} %bitcast.51), channel_id=1, source_target_pairs={{0,32},{32,64},{64,96},{96,128},{128,160},{160,192},{192,224},{1,3... | collective-permute-start | bytes 6291464 | tf_op jit(solution)/shard_map/ppermute | solution.py:13
  16.8 121.3 %collective-permute-start.2 = (f32[256,2048]{1,0:T(8,128)}, f32[256,2048]{1,0:T(8,128)S(1)}, u32[]{:S(2)}, u32[]{:S(2)}) collective-permute-start(f32[256,2048]{1,0:T(8,128)} %bitcast.52), channel_id=1, source_target_pairs={{0,96},{32,128},{64,160},{96,192},{128,224},{1,97},{33,129},{65,16... | collective-permute-start | bytes 6291464 | tf_op jit(solution)/shard_map/ppermute | solution.py:13
  145.9 1061.0 %all-gather.6.cloned.1.call-start = ((), (), s32[]{:S(2)}) async-start(), calls=%async_computation.3 | async-start | bytes 53477376 | tf_op jit(solution)/shard_map/all_gather | solution.py:27
  178.7 1070.2 %all-gather.4.cloned.1.call-start = ((), (), s32[]{:S(2)}) async-start(), calls=%async_computation.2 | async-start | bytes 9437184 | tf_op jit(solution)/shard_map/all_gather | solution.py:29
  1225.7 0.7 copy-start.2
  1248.9 15.4 %copy-start = (f32[768,2048]{1,0:T(8,128)S(1)}, f32[768,2048]{1,0:T(8,128)}, u32[]{:S(2)}) copy-start(f32[768,2048]{1,0:T(8,128)} %all-gather.4.cloned.1.call-done) | copy-start | bytes 18874372
  1261.3 117.8 %collective-permute-start.3 = (f32[256,2048]{0,1:T(8,128)S(1)}, f32[256,2048]{0,1:T(8,128)S(1)}, u32[]{:S(2)}, u32[]{:S(2)}) collective-permute-start(f32[256,2048]{0,1:T(8,128)S(1)} %fusion.15), channel_id=1, source_target_pairs={{32,0},{64,32},{96,64},{128,96},{160,128},{192,160},{224,192},{33,... | collective-permute-start | bytes 6291464 | tf_op jit(solution)/shard_map/ppermute | solution.py:13
  1274.8 104.3 %collective-permute-start.4 = (f32[256,2048]{0,1:T(8,128)S(1)}, f32[256,2048]{0,1:T(8,128)S(1)}, u32[]{:S(2)}, u32[]{:S(2)}) collective-permute-start(f32[256,2048]{0,1:T(8,128)S(1)} %fusion.18), channel_id=1, source_target_pairs={{64,0},{96,32},{128,64},{160,96},{192,128},{224,160},{65,1},{97,33... | collective-permute-start | bytes 6291464 | tf_op jit(solution)/shard_map/ppermute | solution.py:13
  1289.0 115.6 %collective-permute-start.5 = (f32[256,2048]{0,1:T(8,128)S(1)}, f32[256,2048]{0,1:T(8,128)S(1)}, u32[]{:S(2)}, u32[]{:S(2)}) collective-permute-start(f32[256,2048]{0,1:T(8,128)S(1)} %fusion.21), channel_id=1, source_target_pairs={{96,0},{128,32},{160,64},{192,96},{224,128},{97,1},{129,33},{161,6... | collective-permute-start | bytes 6291464 | tf_op jit(solution)/shard_map/ppermute | solution.py:13
Sparse Core Ops, SparseCore 0:
  146.0 32.6 reduce-scatter.1
  180.5 1026.3 all-gather.5
  1225.9 22.9 all-gather.3
